TPU v7x, 32 devices: a whole 2x2x4 slice. The times are simulated.
32 devices in a mesh: section: 2 (over y), tensor: 4 (over x, core), dp: 4 (over z).
Axes of the slice: x: 2, y: 2, z: 4, core: 2. Of those that a mesh axis runs over, the one named last changes fastest.
Arguments:
- hidden: bfloat16 [2, 8, 256, 14336], P('section', 'dp', None, 'tensor'), parts along dimension 1, may hold values from -6 to 6
- down_weight: bfloat16 [2, 14336, 4096], P('section', 'tensor'), may hold values from -0.046875 to 0.046875
- residual: bfloat16 [2, 8, 256, 4096], P('section', 'dp', 'tensor'), parts along dimension 1, may hold values from -6 to 6
- norm_gain: float32 [2, 4096], P('section'), may hold values from 0.1 to 1.9
- qkv_weight: bfloat16 [2, 4096, 5120], P('section', None, 'tensor'), may hold values from -0.09375 to 0.09375
Outputs:
- carried: bfloat16 [2, 8, 256, 4096], P('section', 'dp', 'tensor'), parts along dimension 1
- attention_inputs: bfloat16 [2, 8, 256, 5120], P('section', 'dp', None, 'tensor'), parts along dimension 1
There are 4 independent parts, one for each index of `dp`. A program takes and returns all parts, laid end to end along the dimension named above; an argument that names none is the same for every part. Nothing has to cross between parts.
All inputs are finite; a program needn't handle non-finite values.
Results may differ from a plain program's by a relative error of at most 0.012.
Values may be sent and summed in bfloat16 or wider, within the bound.
A program may use at most 128 MiB of HBM per device.

v0:
```python
import jax
import jax.numpy as jnp
from jax import lax
from jax.sharding import PartitionSpec as P


def shifted(value, axis, steps):
    count = lax.axis_size(axis)
    pairs = [(source, (source + steps) % count) for source in range(count)]
    return lax.ppermute(value, axis, pairs)


def normalize(stream, gain):
    values = stream.astype(jnp.float32)
    mean_square = jnp.mean(values * values, axis=-1, keepdims=True)
    return (values * lax.rsqrt(mean_square + 1e-05) * gain[None, None, :]).astype(jnp.bfloat16)


def per_device(hidden, down_weight, residual, norm_gain, qkv_weight):
    micro_count = hidden.shape[1]
    local_rows = residual.shape[2]
    weight = down_weight[0]
    activations = hidden[0]
    pieces = []
    for batch_index in range(micro_count):
        rows_here = activations[batch_index]

        def batch_term(first_row, row_count, rows_here=rows_here):
            return jnp.dot(rows_here, weight, preferred_element_type=jnp.float32)

        pieces.append(
            lax.psum_scatter(
                batch_term(jnp.int32(0), local_rows * lax.axis_size("tensor")).astype(jnp.bfloat16),
                "tensor",
                scatter_dimension=0,
                tiled=True,
            ).astype(jnp.float32)
        )
    reduced = jnp.stack(pieces)
    stream = (reduced + residual[0].astype(jnp.float32)).astype(jnp.bfloat16)
    gain = norm_gain[0]
    projector = qkv_weight[0]
    gathered = lax.all_gather(stream, "tensor", axis=1, tiled=True)
    arrived = shifted(gathered, "section", 1)
    normed = normalize(arrived, gain)
    projected = jnp.einsum(
        "mtd,dq->mtq", normed, projector, preferred_element_type=jnp.float32
    ).astype(jnp.bfloat16)
    carried = lax.dynamic_slice_in_dim(
        arrived, lax.axis_index("tensor") * local_rows, local_rows, 1
    )
    return (carried[None], projected[None])


def solution(mesh):
    placed = (
        P("section", "dp", None, "tensor"),
        P("section", "tensor", None),
        P("section", "dp", "tensor", None),
        P("section", None),
        P("section", None, "tensor"),
    )
    return jax.shard_map(
        per_device,
        mesh=mesh,
        in_specs=placed,
        out_specs=(P("section", "dp", "tensor", None), P("section", "dp", None, "tensor")),
        check_vma=False,
    )
```

profile of v0, /device:TPU:0, one launch (start us, length us, event | category | flops | bytes accessed | tf_op | source)
XLA Modules:
  0.0 243.9 jit_solution(11271526696843832025)
XLA Ops:
  7.2 0.0 reduce-scatter.5.cloned.1.call-start
  7.2 14.8 %fusion.12 = bf16[256,4096]{1,0:T(8,128)(2,1)} fusion(bf16[1,3584,4096]{2,1,0:T(8,128)(2,1)} %param.6, bf16[1,2,256,3584]{3,2,1,0:T(8,128)(2,1)} %param.5), kind=kOutput, calls=%fused_computation.12 | convolution fusion | flops 7517241344 | bytes 33292288 | tf_op jit(solution)/shard_map/dot_general | solution.py:29
  22.0 0.0 reduce-scatter.5.cloned.1.call-update
  22.1 0.0 copy-start
  22.1 0.0 reduce-scatter.3.cloned.1.call-start
  22.1 15.3 %fusion.9 = bf16[256,4096]{1,0:T(8,128)(2,1)} fusion(bf16[1,3584,4096]{2,1,0:T(8,128)(2,1)} %param.6, bf16[1,2,256,3584]{3,2,1,0:T(8,128)(2,1)} %param.5), kind=kOutput, calls=%fused_computation.11 | convolution fusion | flops 7517241344 | bytes 33292288 | tf_op jit(solution)/shard_map/dot_general | solution.py:29
  37.4 0.0 reduce-scatter.3.cloned.1.call-update
  37.5 0.0 all-gather.2.cloned.1.call-start
  37.5 18.8 %reduce-scatter.5.cloned.1.call-done = bf16[64,4096]{1,0:T(8,128)(2,1)} async-done(((bf16[256,4096]{1,0:T(8,128)(2,1)}), bf16[64,4096]{1,0:T(8,128)(2,1)}) %reduce-scatter.5.cloned.1.call-update) | async-done | bytes 524304 | tf_op jit(solution)/shard_map/reduce_scatter | solution.py:32
  56.4 34.2 %reduce-scatter.3.cloned.1.call-done = bf16[64,4096]{1,0:T(8,128)(2,1)} async-done(((bf16[256,4096]{1,0:T(8,128)(2,1)}), bf16[64,4096]{1,0:T(8,128)(2,1)}) %reduce-scatter.3.cloned.1.call-update) | async-done | bytes 524304 | tf_op jit(solution)/shard_map/reduce_scatter | solution.py:32
  90.5 0.0 copy-done
  90.5 2.4 fusion.28
  92.9 0.0 copy-start.1
  92.9 0.0 all-gather.2.cloned.1.call-update
  93.0 34.6 %all-gather.2.cloned.1.call-done = bf16[2,256,4096]{2,1,0:T(8,128)(2,1)} async-done(((bf16[2,64,4096]{2,1,0:T(8,128)(2,1)}), bf16[2,256,4096]{2,1,0:T(8,128)(2,1)}) %all-gather.2.cloned.1.call-update) | async-done | bytes 4194320 | tf_op jit(solution)/shard_map/all_gather | solution.py:43
  127.6 1.5 collective-permute-start
  129.1 91.6 %collective-permute-done = bf16[2,256,4096]{2,1,0:T(8,128)(2,1)} collective-permute-done((bf16[2,256,4096]{2,1,0:T(8,128)(2,1)}, bf16[2,256,4096]{2,1,0:T(8,128)(2,1)}, u32[]{:S(2)}, u32[]{:S(2)}) %collective-permute-start) | collective-permute-done | bytes 4194336 | tf_op jit(solution)/shard_map/ppermute | solution.py:10
  220.6 3.1 %fusion.6 = f32[2,256]{1,0:T(2,128)S(1)} fusion(bf16[2,256,4096]{2,1,0:T(8,128)(2,1)} %collective-permute-done), kind=kLoop, calls=%fused_computation.8 | loop fusion | flops 6290944 | bytes 4196352 | tf_op jit(solution)/shard_map/reduce_sum | solution.py:15
  223.7 2.3 dynamic-slice_bitcast_fusion
  226.0 0.0 copy-done.1
  226.0 11.3 %fusion.23 = bf16[1,2,256,1280]{3,2,1,0:T(8,128)(2,1)} fusion(bf16[1,4096,1280]{2,1,0:T(8,128)(2,1)} %param.9, bf16[2,256,4096]{2,1,0:T(8,128)(2,1)} %collective-permute-done, f32[4096]{0:T(1024)S(1)} %bitcast.35, f32[2,256]{1,0:T(2,128)S(1)} %add_rsqrt_fusion), kind=kOutput, calls=%fused_computation.16 | convolution fusion | flops 5377753088 | bytes 16009216 | tf_op jit(solution)/shard_map/mtd,dq->mtq/dot_general | solution.py:46
  (1 shorter events, 0.0 us)
Async XLA Ops:
  7.2 49.2 %reduce-scatter.5.cloned.1.call-start = ((), (), s32[]{:S(2)}) async-start(), calls=%async_computation.3 | async-start | bytes 2621440 | tf_op jit(solution)/shard_map/reduce_scatter | solution.py:32
  22.1 68.4 %copy-start = (bf16[1,2,64,4096]{3,2,1,0:T(8,128)(2,1)S(1)}, bf16[1,2,64,4096]{3,2,1,0:T(8,128)(2,1)}, u32[]{:S(2)}) copy-start(bf16[1,2,64,4096]{3,2,1,0:T(8,128)(2,1)} %param.7) | copy-start | bytes 3145732
  22.1 68.4 %reduce-scatter.3.cloned.1.call-start = ((), (), s32[]{:S(2)}) async-start(), calls=%async_computation.2 | async-start | bytes 2621440 | tf_op jit(solution)/shard_map/reduce_scatter | solution.py:32
  37.5 90.1 %all-gather.2.cloned.1.call-start = ((), (), s32[]{:S(2)}) async-start(), calls=%async_computation.4 | async-start | bytes 5242880 | tf_op jit(solution)/shard_map/all_gather | solution.py:43
  92.9 133.1 %copy-start.1 = (f32[1,4096]{1,0:T(1,128)S(1)}, f32[1,4096]{1,0:T(1,128)}, u32[]{:S(2)}) copy-start(f32[1,4096]{1,0:T(1,128)} %param.8) | copy-start | bytes 49156
  127.6 93.0 %collective-permute-start = (bf16[2,256,4096]{2,1,0:T(8,128)(2,1)}, bf16[2,256,4096]{2,1,0:T(8,128)(2,1)}, u32[]{:S(2)}, u32[]{:S(2)}) collective-permute-start(bf16[2,256,4096]{2,1,0:T(8,128)(2,1)} %all-gather.2.cloned.1.call-done), channel_id=1, source_target_pairs={{0,16},{16,0},{1,17},{17,1},{2,18},{18,2},{3,19},{19,3},{4,20},{20... | collective-permute-start | bytes 12582920 | tf_op jit(solution)/shard_map/ppermute | solution.py:10
Sparse Core Ops, SparseCore 0:
  22.2 34.1 reduce-scatter.4
  59.0 31.4 reduce-scatter.2
  93.1 34.4 all-gather.1
where the time goes:
time: 244 us
  waiting for transfers between devices  179 us (73%)
  matrix products  41.5 us (17%)
  between operations  13.8 us (6%)
  other arithmetic  5.51 us (2%)
    ppermute x1, waiting for transfers between devices, shifted(): return lax.ppermute(value, axis, pairs)  91.6 us
    reduce_scatter x2, waiting for transfers between devices, per_device(): lax.psum_scatter(batch_term(jnp.int32(0), local_rows * lax.axis_size('ten...  53 us
    all_gather x1, waiting for transfers between devices, per_device(): gathered = lax.all_gather(stream, 'tensor', axis=1, tiled=True)  34.6 us
    dot_general x2, matrix products, batch_term(): return jnp.dot(rows_here, weight, preferred_element_type=jnp.float32)  30.1 us
    dot_general x1, matrix products, per_device(): jnp.einsum('mtd,dq->mtq', normed, projector, preferred_element_type=jnp.f...  11.3 us
  transfers between devices with their start and end apart: 4, of which 4 were waited for; matrix products, arithmetic and copies ran while one was open for 6% of the time, Pallas kernels for 0%

commit v1 on v0

v1 whole, which is shorter than its diff:
```python
import functools

import jax
import jax.numpy as jnp
from jax import lax
from jax.experimental import pallas as pl
from jax.experimental.pallas import tpu as pltpu
from jax.sharding import PartitionSpec as P

MESH = pl.DeviceIdType.MESH
F32 = jnp.float32
BF16 = jnp.bfloat16
CHUNKS = 8
SLABS = 3
LAG_X, LAG_SUM, LAG_HAND, LAG_PASS, LAG_PROJ = 1, 3, 5, 6, 7


def kernel(
    sections, tensor, hidden, weight, residual, gain, projector,
    carried_out, projected_out,
    rows, slab, qkv, res, own, core_send, core_recv, x_send, x_recv, base, stream, carried, acc, squares, out,
    hidden_sem, slab_sem, qkv_sem, res_sem, carried_sem, out_sem,
    core_ss, core_rs, x_ss, x_rs, y_ss, y_rs, g_ss, g_rs, c_ss, c_rs,
):
    chips = tensor // 2
    chunks, micro, local, width = stream.shape
    features = chunks * width
    depth = rows.shape[-1]
    half = chips * micro * local
    total = 2 * half
    s = lax.axis_index("section")
    t = lax.axis_index("tensor")
    chip, core = t // 2, lax.rem(t, 2)
    sibling = chip * 2 + 1 - core
    following = lax.rem(s + 1, sections)
    previous = lax.rem(s + sections - 1, sections)

    def ahead(j):
        return lax.rem(chip + j, chips)

    def behind(j):
        return lax.rem(chip + chips - j, chips)

    def hidden_copy(side, c, m):
        lane = 1 - core if side == 0 else core
        first = pl.multiple_of((c * 2 + lane) * local, local)
        return pltpu.make_async_copy(
            hidden.at[0, m, pl.ds(first, local), :], rows.at[side, c, m], hidden_sem.at[side, c, m]
        )

    def columns(k):
        return pl.ds(pl.multiple_of(k * width, width), width)

    def slab_copy(k):
        slot = lax.rem(k, SLABS)
        return pltpu.make_async_copy(weight.at[0, :, columns(k)], slab.at[slot], slab_sem.at[slot])

    def qkv_copy(k):
        return pltpu.make_async_copy(projector.at[0, columns(k), :], qkv.at[k], qkv_sem.at[k])

    res_copy = pltpu.make_async_copy(residual.at[0], res, res_sem)

    def carried_copy(k):
        return pltpu.make_async_copy(carried.at[k, t], carried_out.at[0, :, :, columns(k)], carried_sem.at[k])

    def out_copy(b, m):
        return pltpu.make_async_copy(
            out.at[b, m], projected_out.at[0, m, pl.ds(b * local, local), :], out_sem.at[b, m]
        )

    def core_copy(k):
        return pltpu.make_async_remote_copy(
            src_ref=core_send.at[k], dst_ref=core_recv.at[k], send_sem=core_ss.at[k], recv_sem=core_rs.at[k],
            device_id={"tensor": sibling}, device_id_type=MESH,
        )

    def x_copy(k, j):
        return pltpu.make_async_remote_copy(
            src_ref=x_send.at[k, j - 1], dst_ref=x_recv.at[k, j - 1],
            send_sem=x_ss.at[k, j - 1], recv_sem=x_rs.at[k, j - 1],
            device_id={"tensor": ahead(j) * 2 + core}, device_id_type=MESH,
        )

    def y_copy(k):
        return pltpu.make_async_remote_copy(
            src_ref=stream.at[k], dst_ref=carried.at[k, t], send_sem=y_ss.at[k], recv_sem=y_rs.at[k],
            device_id={"section": following}, device_id_type=MESH,
        )

    def gather_copy(k, j, block):
        return pltpu.make_async_remote_copy(
            src_ref=carried.at[k, block], dst_ref=carried.at[k, block],
            send_sem=g_ss.at[k, j - 1], recv_sem=g_rs.at[k, j - 1],
            device_id={"tensor": ahead(j) * 2 + core}, device_id_type=MESH,
        )

    def pass_copy(k, j, block):
        return pltpu.make_async_remote_copy(
            src_ref=carried.at[k, block], dst_ref=carried.at[k, block],
            send_sem=c_ss.at[k, j], recv_sem=c_rs.at[k, j],
            device_id={"tensor": sibling}, device_id_type=MESH,
        )

    for side in range(2):
        for c in range(chips):
            for m in range(micro):
                hidden_copy(side, c, m).start()
        if side == 0:
            slab_copy(0).start()
    res_copy.start()
    for k in range(1, SLABS):
        slab_copy(k).start()

    barrier = pltpu.get_barrier_semaphore()
    pl.semaphore_signal(barrier, inc=1, device_id={"tensor": sibling}, device_id_type=MESH)
    for j in range(1, chips):
        pl.semaphore_signal(barrier, inc=1, device_id={"tensor": ahead(j) * 2 + core}, device_id_type=MESH)
    pl.semaphore_signal(barrier, inc=1, device_id={"section": following}, device_id_type=MESH)
    if sections > 2:
        pl.semaphore_signal(barrier, inc=1, device_id={"section": previous}, device_id_type=MESH)
    pl.semaphore_wait(barrier, chips + (2 if sections > 2 else 1))

    acc[...] = jnp.zeros_like(acc)
    squares[...] = jnp.zeros_like(squares)

    def multiply(side, slot):
        product = jnp.dot(rows[side].reshape(half, depth), slab[slot], preferred_element_type=F32)
        return product.reshape(chips, micro, local, width)

    def step(i, _):
        @pl.when(i < chunks)
        def _():
            slot = lax.rem(i, SLABS)

            @pl.when(i == 0)
            def _():
                for c in range(chips):
                    for m in range(micro):
                        hidden_copy(0, c, m).wait()

            slab_copy(i).wait()
            core_send[i] = multiply(0, slot).astype(BF16)
            core_copy(i).start()

            @pl.when(i == 0)
            def _():
                for c in range(chips):
                    for m in range(micro):
                        hidden_copy(1, c, m).wait()
                res_copy.wait()

            own[lax.rem(i, 2)] = multiply(1, slot)

            @pl.when(i + SLABS < chunks)
            def _():
                slab_copy(i + SLABS).start()

            qkv_copy(i).start()

        k_x = i - LAG_X

        @pl.when((k_x >= 0) & (k_x < chunks))
        def _():
            k = k_x
            slot = lax.rem(k, 2)
            core_copy(k).wait_recv()
            for j in range(1, chips):
                x_send[k, j - 1] = (own[slot, ahead(j)] + core_recv[k, ahead(j)].astype(F32)).astype(BF16)
                x_copy(k, j).start()
            base[k] = own[slot, chip] + core_recv[k, chip].astype(F32) + res[:, :, columns(k)].astype(F32)

        k_sum = i - LAG_SUM

        @pl.when((k_sum >= 0) & (k_sum < chunks))
        def _():
            k = k_sum
            value = base[k]
            for j in range(1, chips):
                x_copy(k, j).wait_recv()
                value = value + x_recv[k, j - 1].astype(F32)
            stream[k] = value.astype(BF16)
            y_copy(k).start()

        k_hand = i - LAG_HAND

        @pl.when((k_hand >= 0) & (k_hand < chunks))
        def _():
            k = k_hand
            y_copy(k).wait_recv()
            for j in range(1, chips):
                gather_copy(k, j, t).start()
            pass_copy(k, 0, t).start()
            carried_copy(k).start()

        k_pass = i - LAG_PASS

        @pl.when((k_pass >= 0) & (k_pass < chunks))
        def _():
            k = k_pass
            for j in range(1, chips):
                block = behind(j) * 2 + core
                gather_copy(k, j, block).wait_recv()
                pass_copy(k, j, block).start()

        k_proj = i - LAG_PROJ

        @pl.when((k_proj >= 0) & (k_proj < chunks))
        def _():
            k = k_proj
            qkv_copy(k).wait()
            for j in range(chips):
                pass_copy(k, j, behind(j) * 2 + 1 - core).wait_recv()
            values = carried[k].reshape(total, width).astype(F32)
            squared = values * values
            part = squared[:, :128]
            for lane in range(128, width, 128):
                part = part + squared[:, lane:lane + 128]
            squares[...] += part
            scaled = (values * gain[:, columns(k)]).astype(BF16)
            acc[...] += jnp.dot(scaled, qkv[k], preferred_element_type=F32)

        return 0

    lax.fori_loop(0, chunks + LAG_PROJ, step, 0)

    block_rows = micro * local
    for b in range(tensor):
        lines = pl.ds(b * block_rows, block_rows)
        mean = jnp.sum(squares[lines, :], axis=-1, keepdims=True) * (1.0 / features)
        value = acc[lines, :] * lax.rsqrt(mean + 1e-05)
        out[b] = value.astype(BF16).reshape(out.shape[1:])
        for m in range(micro):
            out_copy(b, m).start()

    def drain(k, _):
        core_copy(k).wait_send()
        y_copy(k).wait_send()
        carried_copy(k).wait()
        pass_copy(k, 0, t).wait_send()
        for j in range(1, chips):
            x_copy(k, j).wait_send()
            gather_copy(k, j, t).wait_send()
            pass_copy(k, j, behind(j) * 2 + core).wait_send()
        return 0

    lax.fori_loop(0, chunks, drain, 0)
    for b in range(tensor):
        for m in range(micro):
            out_copy(b, m).wait()


def per_device(sections, tensor, hidden, down_weight, residual, norm_gain, qkv_weight):
    _, micro, tokens, depth = hidden.shape
    local, features = residual.shape[2:]
    columns = qkv_weight.shape[2]
    chips = tensor // 2
    chunks = CHUNKS
    width = features // chunks
    dma = pltpu.SemaphoreType.DMA
    anywhere = pl.BlockSpec(memory_space=pl.ANY)
    return pl.pallas_call(
        functools.partial(kernel, sections, tensor),
        out_shape=(
            jax.ShapeDtypeStruct((1, micro, local, features), BF16),
            jax.ShapeDtypeStruct((1, micro, tokens, columns), BF16),
        ),
        in_specs=[anywhere, anywhere, anywhere, pl.BlockSpec(memory_space=pltpu.VMEM), anywhere],
        out_specs=(anywhere, anywhere),
        scratch_shapes=[
            pltpu.VMEM((2, chips, micro, local, depth), BF16),
            pltpu.VMEM((SLABS, depth, width), BF16),
            pltpu.VMEM((chunks, width, columns), BF16),
            pltpu.VMEM((micro, local, features), BF16),
            pltpu.VMEM((2, chips, micro, local, width), F32),
            pltpu.VMEM((chunks, chips, micro, local, width), BF16),
            pltpu.VMEM((chunks, chips, micro, local, width), BF16),
            pltpu.VMEM((chunks, chips - 1, micro, local, width), BF16),
            pltpu.VMEM((chunks, chips - 1, micro, local, width), BF16),
            pltpu.VMEM((chunks, micro, local, width), F32),
            pltpu.VMEM((chunks, micro, local, width), BF16),
            pltpu.VMEM((chunks, tensor, micro, local, width), BF16),
            pltpu.VMEM((micro * tokens, columns), F32),
            pltpu.VMEM((micro * tokens, 128), F32),
            pltpu.VMEM((tensor, micro, local, columns), BF16),
            dma((2, chips, micro)), dma((SLABS,)), dma((chunks,)), dma, dma((chunks,)), dma((tensor, micro)),
            dma((chunks,)), dma((chunks,)),
            dma((chunks, chips - 1)), dma((chunks, chips - 1)),
            dma((chunks,)), dma((chunks,)),
            dma((chunks, chips - 1)), dma((chunks, chips - 1)),
            dma((chunks, chips)), dma((chunks, chips)),
        ],
        compiler_params=pltpu.CompilerParams(
            collective_id=0, has_side_effects=True, vmem_limit_bytes=60 * 1024 * 1024
        ),
    )(hidden, down_weight, residual, norm_gain, qkv_weight)


def solution(mesh):
    placed = (
        P("section", "dp", None, "tensor"),
        P("section", "tensor", None),
        P("section", "dp", "tensor", None),
        P("section", None),
        P("section", None, "tensor"),
    )
    return jax.shard_map(
        functools.partial(per_device, mesh.shape["section"], mesh.shape["tensor"]),
        mesh=mesh,
        in_specs=placed,
        out_specs=(P("section", "dp", "tensor", None), P("section", "dp", None, "tensor")),
        check_vma=False,
    )
```

time: 244 us -> 67 us (0.27)
  waiting for transfers between devices: 179 us -> 0 us
  Pallas kernels: 0 us -> 61.4 us
  matrix products: 41.5 us -> 0 us
  between operations: 13.8 us -> 0.64 us
  other arithmetic: 5.51 us -> 0 us
    ppermute x1 -> x0, waiting for transfers between devices: 91.6 us -> none  [shifted(): return lax.ppermute(value, axis, pairs)]
    pallas_call x0 -> x1, Pallas kernels: none -> 61.4 us  [per_device(): pl.pallas_call(functools.partial(kernel, sections, tensor), out_shape=(ja...]
    reduce_scatter x2 -> x0, waiting for transfers between devices: 53 us -> none  [per_device(): lax.psum_scatter(batch_term(jnp.int32(0), local_rows * lax.axis_size('ten...]
    dot_general x3 -> x0, matrix products: 41.5 us -> none  [the longest x2 30.1 us: batch_term(): return jnp.dot(rows_here, weight, preferred_element_type=jnp.float32)]
    all_gather x1 -> x0, waiting for transfers between devices: 34.6 us -> none  [per_device(): gathered = lax.all_gather(stream, 'tensor', axis=1, tiled=True)]
    unnamed x4 -> x2, local copies, waits for them, and re-layouts: 0.01 us -> 4.74 us
    reduce_sum x1 -> x0, other arithmetic: 3.08 us -> none  [normalize(): mean_square = jnp.mean(values * values, axis=-1, keepdims=True)]
  transfers between devices with their start and end apart: 4 -> 0, of which waited for: 4 -> 0; matrix products, arithmetic and copies ran while one was open for 6% -> 0% of each run, Pallas kernels for 0% -> 0%
where the time goes in v1:
time: 67 us; the launch traced here: 66.7 us
  Pallas kernels  61.4 us (92%)
  local copies, waits for them, and re-layouts  4.74 us (7%)
    pallas_call x1, Pallas kernels, per_device(): pl.pallas_call(functools.partial(kernel, sections, tensor), out_shape=(ja...  61.4 us
    unnamed x2, local copies, waits for them, and re-layouts  4.74 us

profile of v1, /device:TPU:0, one launch (start us, length us, event | category | flops | bytes accessed | tf_op | source)
XLA Modules:
  0.0 66.7 jit_solution(11472576230835417592)
XLA Ops:
  0.6 61.4 %shard_map.68 = (bf16[1,2,64,4096]{3,2,1,0:T(8,128)(2,1)}, bf16[1,2,256,1280]{3,2,1,0:T(8,128)(2,1)}) custom-call(bf16[1,2,256,3584]{3,2,1,0:T(8,128)(2,1)} %hidden.1, bf16[1,3584,4096]{2,1,0:T(8,128)(2,1)} %weight.1, bf16[1,2,64,4096]{3,2,1,0:T(8,128)(2,1)} %residual.1, f32[1,4096]{1,0:T(1,128)} %gain.1, bf16[1,4096,1280]{2,1,0:T(8,128)(2,1)} %projector.1), custom_call_target="tpu_custom_call" | custom-call | tf_op jit(solution)/shard_map/pallas_call | solution.py:261
  62.0 2.3 %copy.9 = bf16[1,2,64,4096]{3,2,1,0:T(8,128)(2,1)} copy(bf16[1,2,64,4096]{3,2,1,0:T(8,128)(2,1)} %get-tuple-element.4) | data formatting | bytes 2097152
  64.3 2.5 %copy.10 = bf16[1,2,256,1280]{3,2,1,0:T(8,128)(2,1)} copy(bf16[1,2,256,1280]{3,2,1,0:T(8,128)(2,1)} %get-tuple-element.5) | data formatting | bytes 2621440

commit v2 on v1

v2 whole, which is shorter than its diff:
```python
import functools

import jax
import jax.numpy as jnp
from jax import lax
from jax.experimental import pallas as pl
from jax.experimental.pallas import tpu as pltpu
from jax.sharding import PartitionSpec as P

MESH = pl.DeviceIdType.MESH
F32 = jnp.float32
BF16 = jnp.bfloat16
CHUNKS = 8
SLABS = 3
LAG_SUM, LAG_HAND, LAG_PASS, LAG_PROJ = 2, 4, 5, 6


def kernel(
    sections, tensor, hidden, weight, residual, gain_in, projector,
    carried_out, projected_out,
    rows, slab, qkv, res, gain, own, core_send, core_recv, x_send, x_recv, base, stream, carried, acc, squares, out,
    hidden_sem, slab_sem, qkv_sem, res_sem, gain_sem, carried_sem, out_sem,
    core_ss, core_rs, x_ss, x_rs, y_ss, y_rs, g_ss, g_rs, c_ss, c_rs,
):
    chips = tensor // 2
    chunks, micro, local, width = stream.shape
    features = chunks * width
    depth = rows.shape[-1]
    half = chips * micro * local
    s = lax.axis_index("section")
    t = lax.axis_index("tensor")
    chip, core = t // 2, lax.rem(t, 2)
    sibling = chip * 2 + 1 - core
    following = lax.rem(s + 1, sections)
    previous = lax.rem(s + sections - 1, sections)

    def ahead(j):
        return lax.rem(chip + j, chips)

    def behind(j):
        return lax.rem(chip + chips - j, chips)

    def hidden_copy(side, c, m):
        lane = 1 - core if side == 0 else core
        first = pl.multiple_of((c * 2 + lane) * local, local)
        return pltpu.make_async_copy(
            hidden.at[0, m, pl.ds(first, local), :], rows.at[side, c, m], hidden_sem.at[side, c, m]
        )

    def columns(k):
        return pl.ds(pl.multiple_of(k * width, width), width)

    def slab_copy(k):
        slot = lax.rem(k, SLABS)
        return pltpu.make_async_copy(weight.at[0, :, columns(k)], slab.at[slot], slab_sem.at[slot])

    def qkv_copy(k):
        return pltpu.make_async_copy(projector.at[0, columns(k), :], qkv.at[k], qkv_sem.at[k])

    res_copy = pltpu.make_async_copy(residual.at[0], res, res_sem)
    gain_copy = pltpu.make_async_copy(gain_in, gain, gain_sem)

    def carried_copy(k):
        return pltpu.make_async_copy(carried.at[k, core, chip], carried_out.at[0, :, :, columns(k)], carried_sem.at[k])

    def out_copy(side, c, m):
        lane = core if side == 0 else 1 - core
        first = pl.multiple_of((c * 2 + lane) * local, local)
        return pltpu.make_async_copy(
            out.at[side, c, m], projected_out.at[0, m, pl.ds(first, local), :], out_sem.at[side, c, m]
        )

    def core_copy(k):
        return pltpu.make_async_remote_copy(
            src_ref=core_send.at[k], dst_ref=core_recv.at[k], send_sem=core_ss.at[k], recv_sem=core_rs.at[k],
            device_id={"tensor": sibling}, device_id_type=MESH,
        )

    def x_copy(k, j):
        return pltpu.make_async_remote_copy(
            src_ref=x_send.at[k, j - 1], dst_ref=x_recv.at[k, j - 1],
            send_sem=x_ss.at[k, j - 1], recv_sem=x_rs.at[k, j - 1],
            device_id={"tensor": ahead(j) * 2 + core}, device_id_type=MESH,
        )

    def y_copy(k):
        return pltpu.make_async_remote_copy(
            src_ref=stream.at[k], dst_ref=carried.at[k, core, chip], send_sem=y_ss.at[k], recv_sem=y_rs.at[k],
            device_id={"section": following}, device_id_type=MESH,
        )

    def gather_copy(k, j, block):
        block = (core, block)
        return pltpu.make_async_remote_copy(
            src_ref=carried.at[k, *block], dst_ref=carried.at[k, *block],
            send_sem=g_ss.at[k, j - 1], recv_sem=g_rs.at[k, j - 1],
            device_id={"tensor": ahead(j) * 2 + core}, device_id_type=MESH,
        )

    def pass_copy(k, j, lane, block):
        block = (lane, block)
        return pltpu.make_async_remote_copy(
            src_ref=carried.at[k, *block], dst_ref=carried.at[k, *block],
            send_sem=c_ss.at[k, j], recv_sem=c_rs.at[k, j],
            device_id={"tensor": sibling}, device_id_type=MESH,
        )

    def hidden_start(side):
        for c in range(chips):
            for m in range(micro):
                hidden_copy(side, c, m).start()

    def hidden_wait(side):
        for c in range(chips):
            for m in range(micro):
                hidden_copy(side, c, m).wait()

    hidden_start(0)
    slab_copy(0).start()

    barrier = pltpu.get_barrier_semaphore()
    pl.semaphore_signal(barrier, inc=1, device_id={"tensor": sibling}, device_id_type=MESH)
    for j in range(1, chips):
        pl.semaphore_signal(barrier, inc=1, device_id={"tensor": ahead(j) * 2 + core}, device_id_type=MESH)
    pl.semaphore_signal(barrier, inc=1, device_id={"section": following}, device_id_type=MESH)
    if sections > 2:
        pl.semaphore_signal(barrier, inc=1, device_id={"section": previous}, device_id_type=MESH)
    pl.semaphore_wait(barrier, chips + (2 if sections > 2 else 1))

    acc[...] = jnp.zeros_like(acc)
    squares[...] = jnp.zeros_like(squares)

    def multiply(side, slot):
        product = jnp.dot(rows[side].reshape(half, depth), slab[slot], preferred_element_type=F32)
        return product.reshape(chips, micro, local, width)

    def project(k, side):
        lane = core if side == 0 else 1 - core
        values = carried[k, lane].reshape(half, width).astype(F32)
        squared = values * values
        part = squared[:, :128]
        for first in range(128, width, 128):
            part = part + squared[:, first:first + 128]
        squares[side] += part
        scaled = (values * gain[:, columns(k)]).astype(BF16)
        acc[side] += jnp.dot(scaled, qkv[k], preferred_element_type=F32)

    def finish(side):
        mean = jnp.sum(squares[side], axis=-1, keepdims=True) * (1.0 / features)
        value = acc[side] * lax.rsqrt(mean + 1e-05)
        out[side] = value.astype(BF16).reshape(out.shape[1:])
        for c in range(chips):
            for m in range(micro):
                out_copy(side, c, m).start()

    def step(i, _):
        @pl.when(i < chunks)
        def _():
            slot = lax.rem(i, SLABS)

            @pl.when(i == 0)
            def _():
                hidden_wait(0)

            slab_copy(i).wait()

            @pl.when(i == 0)
            def _():
                hidden_start(1)
                res_copy.start()
                gain_copy.start()
                for k in range(1, SLABS):
                    slab_copy(k).start()

            core_send[i] = multiply(0, slot).astype(BF16)
            core_copy(i).start()

            @pl.when(i == 0)
            def _():
                hidden_wait(1)
                res_copy.wait()
                gain_copy.wait()

            own[...] = multiply(1, slot)

            @pl.when(i + SLABS < chunks)
            def _():
                slab_copy(i + SLABS).start()

            qkv_copy(i).start()
            core_copy(i).wait_recv()
            for j in range(1, chips):
                x_send[i, j - 1] = (own[ahead(j)] + core_recv[i, ahead(j)].astype(F32)).astype(BF16)
                x_copy(i, j).start()
            base[i] = own[chip] + core_recv[i, chip].astype(F32) + res[:, :, columns(i)].astype(F32)

        k_sum = i - LAG_SUM

        @pl.when((k_sum >= 0) & (k_sum < chunks))
        def _():
            k = k_sum
            value = base[k]
            for j in range(1, chips):
                x_copy(k, j).wait_recv()
                value = value + x_recv[k, j - 1].astype(F32)
            stream[k] = value.astype(BF16)
            y_copy(k).start()

        k_hand = i - LAG_HAND

        @pl.when((k_hand >= 0) & (k_hand < chunks))
        def _():
            k = k_hand
            y_copy(k).wait_recv()
            for j in range(1, chips):
                gather_copy(k, j, chip).start()
            pass_copy(k, 0, core, chip).start()
            carried_copy(k).start()

        k_proj = i - LAG_PROJ

        @pl.when((k_proj >= 0) & (k_proj < chunks))
        def _():
            k = k_proj
            for j in range(chips):
                pass_copy(k, j, 1 - core, behind(j)).wait_recv()
            project(k, 1)

        k_pass = i - LAG_PASS

        @pl.when((k_pass >= 0) & (k_pass < chunks))
        def _():
            k = k_pass
            for j in range(1, chips):
                gather_copy(k, j, behind(j)).wait_recv()
                pass_copy(k, j, core, behind(j)).start()
            qkv_copy(k).wait()
            project(k, 0)

            @pl.when(k == chunks - 1)
            def _():
                finish(0)

        return 0

    lax.fori_loop(0, chunks + LAG_PROJ, step, 0)
    finish(1)

    def drain(k, _):
        core_copy(k).wait_send()
        y_copy(k).wait_send()
        carried_copy(k).wait()
        pass_copy(k, 0, core, chip).wait_send()
        for j in range(1, chips):
            x_copy(k, j).wait_send()
            gather_copy(k, j, chip).wait_send()
            pass_copy(k, j, core, behind(j)).wait_send()
        return 0

    lax.fori_loop(0, chunks, drain, 0)
    for side in range(2):
        for c in range(chips):
            for m in range(micro):
                out_copy(side, c, m).wait()


def per_device(sections, tensor, hidden, down_weight, residual, norm_gain, qkv_weight):
    _, micro, tokens, depth = hidden.shape
    local, features = residual.shape[2:]
    columns = qkv_weight.shape[2]
    chips = tensor // 2
    chunks = CHUNKS
    width = features // chunks
    dma = pltpu.SemaphoreType.DMA
    anywhere = pl.BlockSpec(memory_space=pl.ANY)
    return pl.pallas_call(
        functools.partial(kernel, sections, tensor),
        out_shape=(
            jax.ShapeDtypeStruct((1, micro, local, features), BF16),
            jax.ShapeDtypeStruct((1, micro, tokens, columns), BF16),
        ),
        in_specs=[pl.BlockSpec(memory_space=pltpu.HBM)] * 5,
        out_specs=(anywhere, anywhere),
        scratch_shapes=[
            pltpu.VMEM((2, chips, micro, local, depth), BF16),
            pltpu.VMEM((SLABS, depth, width), BF16),
            pltpu.VMEM((chunks, width, columns), BF16),
            pltpu.VMEM((micro, local, features), BF16),
            pltpu.VMEM((1, features), F32),
            pltpu.VMEM((chips, micro, local, width), F32),
            pltpu.VMEM((chunks, chips, micro, local, width), BF16),
            pltpu.VMEM((chunks, chips, micro, local, width), BF16),
            pltpu.VMEM((chunks, chips - 1, micro, local, width), BF16),
            pltpu.VMEM((chunks, chips - 1, micro, local, width), BF16),
            pltpu.VMEM((chunks, micro, local, width), F32),
            pltpu.VMEM((chunks, micro, local, width), BF16),
            pltpu.VMEM((chunks, 2, chips, micro, local, width), BF16),
            pltpu.VMEM((2, micro * tokens // 2, columns), F32),
            pltpu.VMEM((2, micro * tokens // 2, 128), F32),
            pltpu.VMEM((2, chips, micro, local, columns), BF16),
            dma((2, chips, micro)), dma((SLABS,)), dma((chunks,)), dma, dma, dma((chunks,)), dma((2, chips, micro)),
            dma((chunks,)), dma((chunks,)),
            dma((chunks, chips - 1)), dma((chunks, chips - 1)),
            dma((chunks,)), dma((chunks,)),
            dma((chunks, chips - 1)), dma((chunks, chips - 1)),
            dma((chunks, chips)), dma((chunks, chips)),
        ],
        compiler_params=pltpu.CompilerParams(
            collective_id=0, has_side_effects=True, vmem_limit_bytes=50 * 1024 * 1024
        ),
    )(hidden, down_weight, residual, norm_gain, qkv_weight)


def solution(mesh):
    placed = (
        P("section", "dp", None, "tensor"),
        P("section", "tensor", None),
        P("section", "dp", "tensor", None),
        P("section", None),
        P("section", None, "tensor"),
    )
    return jax.shard_map(
        functools.partial(per_device, mesh.shape["section"], mesh.shape["tensor"]),
        mesh=mesh,
        in_specs=placed,
        out_specs=(P("section", "dp", "tensor", None), P("section", "dp", None, "tensor")),
        check_vma=False,
    )
```

time: 67 us -> 63.3 us (0.945)
  Pallas kernels: 61.4 us -> 58.5 us
  local copies, waits for them, and re-layouts: 4.74 us -> 3.96 us
    pallas_call x1, Pallas kernels: 61.4 us -> 58.5 us  [per_device(): pl.pallas_call(functools.partial(kernel, sections, tensor), out_shape=(ja...]
    unnamed x2 -> x6, local copies, waits for them, and re-layouts: 4.74 us -> 3.96 us
where the time goes in v2:
time: 63.3 us; the launch traced here: 63.1 us
  Pallas kernels  58.5 us (92%)
  local copies, waits for them, and re-layouts  3.96 us (6%)
  between operations  0.65 us (1%)
    pallas_call x1, Pallas kernels, per_device(): pl.pallas_call(functools.partial(kernel, sections, tensor), out_shape=(ja...  58.5 us
    unnamed x6, local copies, waits for them, and re-layouts  3.96 us

profile of v2, /device:TPU:0, one launch (start us, length us, event | category | flops | bytes accessed | tf_op | source)
XLA Modules:
  0.0 63.1 jit_solution(6477234684235114468)
XLA Ops:
  0.6 0.0 copy-start
  0.6 1.2 %copy-done = bf16[1,2,64,4096]{3,2,1,0:T(8,128)(2,1)S(1)} copy-done((bf16[1,2,64,4096]{3,2,1,0:T(8,128)(2,1)S(1)}, bf16[1,2,64,4096]{3,2,1,0:T(8,128)(2,1)}, u32[]{:S(2)}) %copy-start) | copy-done | bytes 1048600
  1.9 0.0 copy-start.1
  1.9 0.7 %copy-done.1 = f32[1,4096]{1,0:T(1,128)S(1)} copy-done((f32[1,4096]{1,0:T(1,128)S(1)}, f32[1,4096]{1,0:T(1,128)}, u32[]{:S(2)}) %copy-start.1) | copy-done | bytes 16408
  2.6 58.5 %shard_map.68 = (bf16[1,2,64,4096]{3,2,1,0:T(8,128)(2,1)S(1)}, bf16[1,2,256,1280]{3,2,1,0:T(8,128)(2,1)S(1)}) custom-call(bf16[1,2,256,3584]{3,2,1,0:T(8,128)(2,1)} %hidden.1, bf16[1,3584,4096]{2,1,0:T(8,128)(2,1)} %weight.1, bf16[1,2,64,4096]{3,2,1,0:T(8,128)(2,1)S(1)} %copy-done, f32[1,4096]{1,0:T(1,128)S(1)} %copy-done.1, bf16[1,4096,1280]{2,1,0:T(8,128)(2,1)} %projector.1), custom_call_target="tpu_custom_call" | custom-call | tf_op jit(solution)/shard_map/pallas_call | solution.py:276
  61.1 1.0 %copy.9 = bf16[1,2,64,4096]{3,2,1,0:T(8,128)(2,1)} copy(bf16[1,2,64,4096]{3,2,1,0:T(8,128)(2,1)S(1)} %get-tuple-element.4) | data formatting | bytes 2097152
  62.0 1.1 %copy.10 = bf16[1,2,256,1280]{3,2,1,0:T(8,128)(2,1)} copy(bf16[1,2,256,1280]{3,2,1,0:T(8,128)(2,1)S(1)} %get-tuple-element.5) | data formatting | bytes 2621440
Async XLA Ops:
  0.6 1.2 %copy-start = (bf16[1,2,64,4096]{3,2,1,0:T(8,128)(2,1)S(1)}, bf16[1,2,64,4096]{3,2,1,0:T(8,128)(2,1)}, u32[]{:S(2)}) copy-start(bf16[1,2,64,4096]{3,2,1,0:T(8,128)(2,1)} %residual.1) | copy-start | bytes 3145732
  1.9 0.7 %copy-start.1 = (f32[1,4096]{1,0:T(1,128)S(1)}, f32[1,4096]{1,0:T(1,128)}, u32[]{:S(2)}) copy-start(f32[1,4096]{1,0:T(1,128)} %gain_in.1) | copy-start | bytes 49156

commit v3 on v2

--- a/solution.py
+++ b/solution.py
@@ -50,9 +50,16 @@
     def columns(k):
         return pl.ds(pl.multiple_of(k * width, width), width)
 
-    def slab_copy(k):
+    def slab_copy(k, part):
         slot = lax.rem(k, SLABS)
-        return pltpu.make_async_copy(weight.at[0, :, columns(k)], slab.at[slot], slab_sem.at[slot])
+        lines = pl.ds(part * (depth // 2), depth // 2)
+        return pltpu.make_async_copy(
+            weight.at[0, lines, columns(k)], slab.at[slot, lines], slab_sem.at[slot, part]
+        )
+
+    def slab_start(k):
+        for part in range(2):
+            slab_copy(k, part).start()
 
     def qkv_copy(k):
         return pltpu.make_async_copy(projector.at[0, columns(k), :], qkv.at[k], qkv_sem.at[k])
@@ -116,7 +123,7 @@
                 hidden_copy(side, c, m).wait()
 
     hidden_start(0)
-    slab_copy(0).start()
+    slab_start(0)
 
     barrier = pltpu.get_barrier_semaphore()
     pl.semaphore_signal(barrier, inc=1, device_id={"tensor": sibling}, device_id_type=MESH)
@@ -130,8 +137,11 @@
     acc[...] = jnp.zeros_like(acc)
     squares[...] = jnp.zeros_like(squares)
 
-    def multiply(side, slot):
-        product = jnp.dot(rows[side].reshape(half, depth), slab[slot], preferred_element_type=F32)
+    def multiply(side, slot, part):
+        lines = slice(part * (depth // 2), (part + 1) * (depth // 2))
+        product = jnp.dot(
+            rows[side, ..., lines].reshape(half, depth // 2), slab[slot, lines], preferred_element_type=F32
+        )
         return product.reshape(chips, micro, local, width)
 
     def project(k, side):
@@ -162,7 +172,7 @@
             def _():
                 hidden_wait(0)
 
-            slab_copy(i).wait()
+            slab_copy(i, 0).wait()
 
             @pl.when(i == 0)
             def _():
@@ -170,9 +180,11 @@
                 res_copy.start()
                 gain_copy.start()
                 for k in range(1, SLABS):
-                    slab_copy(k).start()
-
-            core_send[i] = multiply(0, slot).astype(BF16)
+                    slab_start(k)
+
+            own[...] = multiply(0, slot, 0)
+            slab_copy(i, 1).wait()
+            core_send[i] = (own[...] + multiply(0, slot, 1)).astype(BF16)
             core_copy(i).start()
 
             @pl.when(i == 0)
@@ -181,11 +193,11 @@
                 res_copy.wait()
                 gain_copy.wait()
 
-            own[...] = multiply(1, slot)
+            own[...] = multiply(1, slot, 0) + multiply(1, slot, 1)
 
             @pl.when(i + SLABS < chunks)
             def _():
-                slab_copy(i + SLABS).start()
+                slab_start(i + SLABS)
 
             qkv_copy(i).start()
             core_copy(i).wait_recv()
@@ -298,7 +310,7 @@
             pltpu.VMEM((2, micro * tokens // 2, columns), F32),
             pltpu.VMEM((2, micro * tokens // 2, 128), F32),
             pltpu.VMEM((2, chips, micro, local, columns), BF16),
-            dma((2, chips, micro)), dma((SLABS,)), dma((chunks,)), dma, dma, dma((chunks,)), dma((2, chips, micro)),
+            dma((2, chips, micro)), dma((SLABS, 2)), dma((chunks,)), dma, dma, dma((chunks,)), dma((2, chips, micro)),
             dma((chunks,)), dma((chunks,)),
             dma((chunks, chips - 1)), dma((chunks, chips - 1)),
             dma((chunks,)), dma((chunks,)),

time: 63.3 us -> 62.8 us (level)
  no operation moved by 1% of the time
where the time goes in v3:
time: 62.8 us; the launch traced here: 62.6 us
  Pallas kernels  58 us (92%)
  local copies, waits for them, and re-layouts  3.96 us (6%)
  between operations  0.65 us (1%)
    pallas_call x1, Pallas kernels, per_device(): pl.pallas_call(functools.partial(kernel, sections, tensor), out_shape=(ja...  58 us
    unnamed x6, local copies, waits for them, and re-layouts  3.96 us

profile of v3, /device:TPU:0, one launch (start us, length us, event | category | flops | bytes accessed | tf_op | source)
XLA Modules:
  0.0 62.6 jit_solution(7405381729580226951)
XLA Ops:
  0.6 0.0 copy-start
  0.6 1.2 %copy-done = bf16[1,2,64,4096]{3,2,1,0:T(8,128)(2,1)S(1)} copy-done((bf16[1,2,64,4096]{3,2,1,0:T(8,128)(2,1)S(1)}, bf16[1,2,64,4096]{3,2,1,0:T(8,128)(2,1)}, u32[]{:S(2)}) %copy-start) | copy-done | bytes 1048600
  1.9 0.0 copy-start.1
  1.9 0.7 %copy-done.1 = f32[1,4096]{1,0:T(1,128)S(1)} copy-done((f32[1,4096]{1,0:T(1,128)S(1)}, f32[1,4096]{1,0:T(1,128)}, u32[]{:S(2)}) %copy-start.1) | copy-done | bytes 16408
  2.6 58.0 %shard_map.68 = (bf16[1,2,64,4096]{3,2,1,0:T(8,128)(2,1)S(1)}, bf16[1,2,256,1280]{3,2,1,0:T(8,128)(2,1)S(1)}) custom-call(bf16[1,2,256,3584]{3,2,1,0:T(8,128)(2,1)} %hidden.1, bf16[1,3584,4096]{2,1,0:T(8,128)(2,1)} %weight.1, bf16[1,2,64,4096]{3,2,1,0:T(8,128)(2,1)S(1)} %copy-done, f32[1,4096]{1,0:T(1,128)S(1)} %copy-done.1, bf16[1,4096,1280]{2,1,0:T(8,128)(2,1)} %projector.1), custom_call_target="tpu_custom_call" | custom-call | tf_op jit(solution)/shard_map/pallas_call | solution.py:288
  60.5 1.0 %copy.9 = bf16[1,2,64,4096]{3,2,1,0:T(8,128)(2,1)} copy(bf16[1,2,64,4096]{3,2,1,0:T(8,128)(2,1)S(1)} %get-tuple-element.4) | data formatting | bytes 2097152
  61.5 1.1 %copy.10 = bf16[1,2,256,1280]{3,2,1,0:T(8,128)(2,1)} copy(bf16[1,2,256,1280]{3,2,1,0:T(8,128)(2,1)S(1)} %get-tuple-element.5) | data formatting | bytes 2621440
Async XLA Ops:
  0.6 1.2 %copy-start = (bf16[1,2,64,4096]{3,2,1,0:T(8,128)(2,1)S(1)}, bf16[1,2,64,4096]{3,2,1,0:T(8,128)(2,1)}, u32[]{:S(2)}) copy-start(bf16[1,2,64,4096]{3,2,1,0:T(8,128)(2,1)} %residual.1) | copy-start | bytes 3145732
  1.9 0.7 %copy-start.1 = (f32[1,4096]{1,0:T(1,128)S(1)}, f32[1,4096]{1,0:T(1,128)}, u32[]{:S(2)}) copy-start(f32[1,4096]{1,0:T(1,128)} %gain_in.1) | copy-start | bytes 49156
